TPU v7x, 32 devices: a whole 2x2x4 slice. The times are simulated.
32 devices in a mesh: boot: 2 (over x), samp: 16 (over z, y, core).
Axes of the slice: x: 2, y: 2, z: 4, core: 2. Of those that a mesh axis runs over, the one named last changes fastest.
Arguments:
- dosage: bfloat16 [32384, 512], P('samp'), may hold values from 0 to 2, as said below
- residuals: bfloat16 [32384, 1280], P('samp', 'boot'), may hold values from -300 to 300
- maf_bin: int32 [512], replicated, may hold values from 0 to 63
- gene_map: int32 [512], replicated, may hold values from 0 to 31, never falling along the last dimension, each value on 1 to 32 neighbouring positions
- gene_order: int32 [32], replicated, may hold values from 0 to 31, each once
Outputs:
- calibrated: float32 [32, 1280], P('samp', 'boot')
Inputs may be any that keep to these rules, and one draw needn't show every extreme that they name: `dosage`: allele counts 0, 1 or 2. `gene_map`: never falling along the variants; each gene holds 1 to 32 consecutive variants, one gene exactly 32. `gene_order`: each gene once.
All inputs are finite; a program needn't handle non-finite values.
Results may differ from a plain program's by a relative error of at most 0.0003.
Values sent between devices are 32-bit elements; how exact they have to be, the bound alone decides.
A program may use at most 64 MiB of HBM per device.

v0:
```python
import math
import jax
import jax.numpy as jnp
from jax import lax
from jax.sharding import PartitionSpec as P

GENE_DEV = 2
RHOS = 11
MAF_BINS = 64
EPSILON = 1e-05


def variant_weights(maf_bin):
    levels = jnp.arange(MAF_BINS, dtype=jnp.float32)
    weight_table = (1.0 - 0.05 * (levels + 0.5) / MAF_BINS) ** 24
    matches = maf_bin[:, None] == jnp.arange(MAF_BINS, dtype=jnp.int32)[None, :]
    return jnp.sum(
        jnp.where(matches, weight_table[None, :], jnp.zeros_like(weight_table)[None, :]), axis=1
    )


def sample_product(dose_part, residuals):
    return lax.dot_general(
        dose_part, residuals, (((0,), (0,)), ((), ())), preferred_element_type=jnp.float32
    )


def shards(dosage, residuals, maf_bin, gene_map, gene_order):
    sample_total = dosage.shape[0] * lax.axis_size("samp")
    scaling = variant_weights(maf_bin) / math.sqrt(sample_total)
    my_index = lax.axis_index("samp")
    partial_value = sample_product(dosage, residuals) * scaling[:, None]
    scores = lax.psum(partial_value, "samp")
    owned_genes = lax.dynamic_slice_in_dim(gene_order, my_index * GENE_DEV, GENE_DEV)
    member = (owned_genes[:, None] == gene_map[None, :]).astype(jnp.float32)
    stacked = jnp.concatenate([scores, scores * scores], axis=1)
    gene_sums = jnp.dot(
        member, stacked, precision=lax.Precision.HIGHEST, preferred_element_type=jnp.float32
    )
    boot_local = residuals.shape[1]
    burden = gene_sums[:, :boot_local]
    skat = gene_sums[:, boot_local:]
    rho_grid = jnp.arange(RHOS, dtype=jnp.float32) / (RHOS - 1)
    mixtures = (1.0 - rho_grid)[None, :, None] * skat[:, None, :] + rho_grid[None, :, None] * (
        burden * burden
    )[:, None, :]
    boot_total = boot_local * lax.axis_size("boot")
    first_sum, square_sum = lax.psum(
        (jnp.sum(mixtures, axis=2), jnp.sum(mixtures * mixtures, axis=2)), "boot"
    )
    center = first_sum / boot_total
    spread = square_sum / boot_total - center * center
    deviation = mixtures - center[:, :, None]
    zscore = deviation / jnp.sqrt(spread[:, :, None] + EPSILON)
    return jnp.max(zscore, axis=1)


def solution(mesh):
    placed = (P("samp", None), P("samp", "boot"), P(), P(), P())
    return jax.shard_map(
        shards, mesh=mesh, in_specs=placed, out_specs=P("samp", "boot"), check_vma=False
    )
```

profile of v0, /device:TPU:0, one launch (start us, length us, event | category | flops | bytes accessed | tf_op | source)
XLA Modules:
  0.0 128.8 jit_solution(401770869329293279)
XLA Ops:
  6.5 0.0 copy-start
  6.5 0.0 all-reduce.3.cloned.1.call-start
  6.6 0.9 select_reduce_fusion
  7.5 0.8 copy-done
  8.3 0.0 copy-start.3
  8.3 4.5 %convolution_multiply_fusion = f32[512,640]{1,0:T(8,128)} fusion(bf16[2024,512]{1,0:T(8,128)(2,1)} %param.5, bf16[2024,640]{1,0:T(8,128)(2,1)S(1)} %copy-done, f32[512]{0:T(512)S(1)} %broadcast_multiply_fusion.1), kind=kOutput, calls=%fused_computation.4 | convolution fusion | flops 1326776320 | bytes 5976064 | tf_op jit(solution)/shard_map/dot_general | solution.py:23
  12.8 0.0 all-reduce.3.cloned.1.call-update
  12.8 0.0 copy-start.2
  12.8 0.0 copy-done.3
  12.9 0.1 dynamic_slice.3
  12.9 96.9 %all-reduce.3.cloned.1.call-done = f32[512,640]{1,0:T(8,128)} async-done(((f32[512,640]{1,0:T(8,128)}), f32[512,640]{1,0:T(8,128)}) %all-reduce.3.cloned.1.call-update) | async-done | bytes 1310736 | tf_op jit(solution)/shard_map/psum | solution.py:33
  109.8 0.0 copy-start.1
  109.8 1.9 %mul.96 = f32[512,640]{1,0:T(8,128)S(1)} multiply(f32[512,640]{1,0:T(8,128)} %all-reduce.3.cloned.1.call-done, f32[512,640]{1,0:T(8,128)} %all-reduce.3.cloned.1.call-done) | non-fusion elementwise | flops 327680 | bytes 3932160 | tf_op jit(solution)/shard_map/mul | solution.py:36
  111.7 0.0 copy-done.2
  111.8 0.1 copy-done.1
  111.9 1.0 fusion
  112.9 0.2 fusion.5
  113.1 8.1 %all-reduce = (f32[2,11]{0,1:T(8,128)S(1)}, f32[2,11]{0,1:T(8,128)S(1)}) all-reduce(f32[2,11]{0,1:T(8,128)S(1)} %get-tuple-element.6, f32[2,11]{0,1:T(8,128)S(1)} %get-tuple-element.5), channel_id=1, replica_groups=mesh['boot'=2,'samp'=16] {'boot'}, use_global_device_ids=true, to_apply=%region_5.6 | all-reduce | flops 44 | bytes 352 | tf_op jit(solution)/shard_map/psum | solution.py:48
  121.2 0.7 fusion.4
  (5 shorter events, 0.1 us)
Async XLA Ops:
  6.5 1.7 %copy-start = (bf16[2024,640]{1,0:T(8,128)(2,1)S(1)}, bf16[2024,640]{1,0:T(8,128)(2,1)}, u32[]{:S(2)}) copy-start(bf16[2024,640]{1,0:T(8,128)(2,1)} %param.6) | copy-start | bytes 7772164
  6.5 103.3 %all-reduce.3.cloned.1.call-start = ((), (), s32[]{:S(2)}) async-start(), calls=%async_computation | async-start | bytes 2621440 | tf_op jit(solution)/shard_map/psum | solution.py:33
  8.3 4.6 %copy-start.3 = (s32[32]{0:T(128)S(1)}, s32[32]{0:T(128)}, u32[]{:S(2)}) copy-start(s32[32]{0:T(128)} %param.9) | copy-start | bytes 388
  12.8 98.9 %copy-start.2 = (s32[512]{0:T(512)S(1)}, s32[512]{0:T(512)}, u32[]{:S(2)}) copy-start(s32[512]{0:T(512)} %param.8) | copy-start | bytes 6148
  109.8 2.1 %copy-start.1 = (f32[512,640]{1,0:T(8,128)S(1)}, f32[512,640]{1,0:T(8,128)}, u32[]{:S(2)}) copy-start(f32[512,640]{1,0:T(8,128)} %all-reduce.3.cloned.1.call-done) | copy-start | bytes 3932164
Sparse Core Ops, SparseCore 0:
  12.9 96.7 all-reduce.2
where the time goes:
time: 129 us
  waiting for transfers between devices  96.9 us (75%)
  between operations  13.4 us (10%)
  blocking collectives  8.14 us (6%)
  matrix products  5.49 us (4%)
  other arithmetic  3.86 us (3%)
    psum x1, waiting for transfers between devices, shards(): scores = lax.psum(partial_value, 'samp')  96.9 us
    psum x1, blocking collectives, shards(): lax.psum((jnp.sum(mixtures, axis=2), jnp.sum(mixtures * mixtures, axis=2)...  8.14 us
    dot_general x1, matrix products, sample_product(): lax.dot_general(dose_part, residuals, (((0,), (0,)), ((), ())), preferred...  4.52 us
  transfers between devices with their start and end apart: 1, of which 1 were waited for; matrix products, arithmetic and copies ran while one was open for 0% of the time, Pallas kernels for 0%

commit v1 on v0

--- a/solution.py
+++ b/solution.py
@@ -30,7 +30,7 @@
     scaling = variant_weights(maf_bin) / math.sqrt(sample_total)
     my_index = lax.axis_index("samp")
     partial_value = sample_product(dosage, residuals) * scaling[:, None]
-    scores = lax.psum(partial_value, "samp")
+    scores = jnp.sum(lax.all_gather(partial_value, "samp"), axis=0)
     owned_genes = lax.dynamic_slice_in_dim(gene_order, my_index * GENE_DEV, GENE_DEV)
     member = (owned_genes[:, None] == gene_map[None, :]).astype(jnp.float32)
     stacked = jnp.concatenate([scores, scores * scores], axis=1)

time: 129 us -> 153 us (1.19)
  waiting for transfers between devices: 96.9 us -> 112 us
  other arithmetic: 3.86 us -> 12.8 us
    all_gather x0 -> x1, waiting for transfers between devices: none -> 112 us  [shards(): scores = jnp.sum(lax.all_gather(partial_value, 'samp'), axis=0)]
    psum x1 -> x0, waiting for transfers between devices: 96.9 us -> none  [shards(): scores = lax.psum(partial_value, 'samp')]
    reduce_sum x0 -> x1, other arithmetic: none -> 8.91 us  [shards(): scores = jnp.sum(lax.all_gather(partial_value, 'samp'), axis=0)]
where the time goes in v1:
time: 153 us; the launch traced here: 152 us
  waiting for transfers between devices  112 us (73%)
  between operations  13.4 us (9%)
  other arithmetic  12.8 us (8%)
  blocking collectives  8.06 us (5%)
  matrix products  5.46 us (4%)
    all_gather x1, waiting for transfers between devices, shards(): scores = jnp.sum(lax.all_gather(partial_value, 'samp'), axis=0)  112 us
    reduce_sum x1, other arithmetic, shards(): scores = jnp.sum(lax.all_gather(partial_value, 'samp'), axis=0)  8.91 us
    psum x1, blocking collectives, shards(): lax.psum((jnp.sum(mixtures, axis=2), jnp.sum(mixtures * mixtures, axis=2)...  8.06 us
    dot_general x1, matrix products, sample_product(): lax.dot_general(dose_part, residuals, (((0,), (0,)), ((), ())), preferred...  4.5 us
  transfers between devices with their start and end apart: 1, of which 1 were waited for; matrix products, arithmetic and copies ran while one was open for 0% of the time, Pallas kernels for 0%

profile of v1, /device:TPU:0, one launch (start us, length us, event | category | flops | bytes accessed | tf_op | source)
XLA Modules:
  0.0 152.3 jit_solution(2033274449311123063)
XLA Ops:
  6.5 0.0 copy-start
  6.5 0.0 all-gather.3.cloned.1.call-start
  6.6 0.9 select_reduce_fusion
  7.5 0.8 copy-done
  8.3 0.0 copy-start.3
  8.3 4.5 %convolution_multiply_fusion = f32[512,640]{1,0:T(8,128)} fusion(bf16[2024,512]{1,0:T(8,128)(2,1)} %param.5, bf16[2024,640]{1,0:T(8,128)(2,1)S(1)} %copy-done, f32[512]{0:T(512)S(1)} %broadcast_multiply_fusion.1), kind=kOutput, calls=%fused_computation.4 | convolution fusion | flops 1326776320 | bytes 5976064 | tf_op jit(solution)/shard_map/dot_general | solution.py:23
  12.8 0.0 all-gather.3.cloned.1.call-update
  12.8 0.0 copy-done.3
  12.8 0.1 dynamic_slice.3
  12.9 111.5 %all-gather.3.cloned.1.call-done = f32[8192,640]{1,0:T(8,128)} async-done(((f32[512,640]{1,0:T(8,128)}), f32[8192,640]{1,0:T(8,128)}) %all-gather.3.cloned.1.call-update) | async-done | bytes 20971536 | tf_op jit(solution)/shard_map/all_gather | solution.py:33
  124.5 8.9 %reduce_sum.37 = f32[512,640]{1,0:T(8,128)} reduce(f32[16,512,640]{2,1,0:T(8,128)} %bitcast.3, f32[]{:T(128)} %constant.10.clone.1), dimensions={0}, to_apply=%region_1.2 | reduce | flops 4915200 | bytes 22282244 | tf_op jit(solution)/shard_map/reduce_sum | solution.py:33
  133.4 0.0 copy-start.1
  133.4 0.0 copy-start.2
  133.4 1.9 %mul.96 = f32[512,640]{1,0:T(8,128)S(1)} multiply(f32[512,640]{1,0:T(8,128)} %reduce_sum.37, f32[512,640]{1,0:T(8,128)} %reduce_sum.37) | non-fusion elementwise | flops 327680 | bytes 3932160 | tf_op jit(solution)/shard_map/mul | solution.py:36
  135.3 0.1 copy-done.1
  135.5 0.0 copy-done.2
  135.5 1.0 fusion
  136.4 0.2 fusion.5
  136.7 8.1 %all-reduce = (f32[2,11]{0,1:T(8,128)S(1)}, f32[2,11]{0,1:T(8,128)S(1)}) all-reduce(f32[2,11]{0,1:T(8,128)S(1)} %get-tuple-element.6, f32[2,11]{0,1:T(8,128)S(1)} %get-tuple-element.5), channel_id=1, replica_groups=mesh['boot'=2,'samp'=16] {'boot'}, use_global_device_ids=true, to_apply=%region_5.6 | all-reduce | flops 44 | bytes 352 | tf_op jit(solution)/shard_map/psum | solution.py:48
  144.7 0.7 fusion.4
  (5 shorter events, 0.1 us)
Async XLA Ops:
  6.5 1.7 %copy-start = (bf16[2024,640]{1,0:T(8,128)(2,1)S(1)}, bf16[2024,640]{1,0:T(8,128)(2,1)}, u32[]{:S(2)}) copy-start(bf16[2024,640]{1,0:T(8,128)(2,1)} %param.6) | copy-start | bytes 7772164
  6.5 117.9 %all-gather.3.cloned.1.call-start = ((), (), s32[]{:S(2)}) async-start(), calls=%async_computation | async-start | bytes 22282240 | tf_op jit(solution)/shard_map/all_gather | solution.py:33
  8.3 4.5 %copy-start.3 = (s32[32]{0:T(128)S(1)}, s32[32]{0:T(128)}, u32[]{:S(2)}) copy-start(s32[32]{0:T(128)} %param.9) | copy-start | bytes 388
  133.4 2.1 %copy-start.1 = (f32[512,640]{1,0:T(8,128)S(1)}, f32[512,640]{1,0:T(8,128)}, u32[]{:S(2)}) copy-start(f32[512,640]{1,0:T(8,128)} %reduce_sum.37) | copy-start | bytes 3932164
  133.4 2.1 %copy-start.2 = (s32[512]{0:T(512)S(1)}, s32[512]{0:T(512)}, u32[]{:S(2)}) copy-start(s32[512]{0:T(512)} %param.8) | copy-start | bytes 6148
Sparse Core Ops, SparseCore 0:
  12.9 111.4 all-gather.2
